TPU v7x, 256 devices: a whole 4x4x8 slice. The times are simulated.
256 devices in a mesh: space: 64 (over z, y, core), rhs: 4 (over x).
Axes of the slice: x: 4, y: 4, z: 8, core: 2. Of those that a mesh axis runs over, the one named last changes fastest.
Arguments:
- rhs_vec: float32 [64, 65536], P('rhs', 'space'), may hold values from -40 to 40
- self_coef: float32 [65536], P('space'), may hold values from 2 to 4
- near_mats: bfloat16 [512, 8, 128, 128], P('space'), may hold values from -0.1875 to 0.1875
- near_ids: int32 [512, 8], P('space'), may hold values from 0 to 511, as said below
- near_count: int32 [512], P('space'), may hold values from 3 to 8, as said below
- interp: bfloat16 [512, 128, 32], P('space'), may hold values from -0.5 to 0.5
- skel_idx: int32 [512, 32], P('space'), may hold values from 0 to 127, as said below
- coupling: bfloat16 [16384, 4, 4096], P('space', 'rhs'), may hold values from -0.0234375 to 0.0234375
- diag_prec: float32 [65536], P('space'), may hold values from 1.5 to 4
- low_rank: float32 [65536, 512], P('space'), may hold values from -0.010481569 to 0.010481569
Outputs:
- solution: float32 [64, 65536], P('rhs', 'space')
Inputs may be any that keep to these rules, and one draw needn't show every extreme that they name: `near_ids`: slot 0 of each block names the block itself, slot 1 a block of the region before it (of its own region for the first region), slot 2 a block of the region after it (of its own region for the last region); every entry names a block of the same 8-block region or of the region before or after it. `near_count`: some regions use all 8 slots in every block. `skel_idx`: each row holds 32 distinct panel numbers of its block, rising.
All inputs are finite; a program needn't handle non-finite values.
Results may differ from a plain program's by a relative error of at most 0.001.
Values may be sent and summed in bfloat16 or wider, within the bound.
A program may use at most 64 MiB of HBM per device.

v0:
```python
import jax
import jax.numpy as jnp
from jax import lax
from jax.sharding import PartitionSpec as P

HIGH = lax.Precision.HIGHEST
EPS = 1e-06


def padded(cells, sides, width):
    for axis, dim in sides:
        count = lax.axis_size(axis)
        ends = count - 1
        head = lax.slice_in_dim(cells, 0, width, axis=dim)
        tail = lax.slice_in_dim(cells, cells.shape[dim] - width, cells.shape[dim], axis=dim)
        cells = jnp.concatenate(
            [
                lax.ppermute(tail, axis, [(i, (i + 1) % count) for i in range(ends)]),
                cells,
                lax.ppermute(head, axis, [((i + 1) % count, i) for i in range(ends)]),
            ],
            axis=dim,
        )
    return cells


def givens_pair(start_len, diag_one, below_one, upper_two, diag_two, below_two):
    radius_one = jnp.sqrt(diag_one * diag_one + below_one * below_one)
    cos_one = diag_one / radius_one
    sin_one = below_one / radius_one
    upper = cos_one * upper_two + sin_one * diag_two
    lower = cos_one * diag_two - sin_one * upper_two
    radius_two = jnp.sqrt(lower * lower + below_two * below_two)
    step_two = lower / radius_two * (-sin_one * start_len) / radius_two
    step_one = (cos_one * start_len - upper * step_two) / radius_one
    return (step_one, step_two)


def column_sum(values):
    return jnp.sum(values, axis=1)


def on_device(
    rhs_vec,
    self_coef,
    near_mats,
    near_ids,
    near_count,
    interp,
    skel_idx,
    coupling,
    diag_prec,
    low_rank,
):
    excitations, panels = rhs_vec.shape
    block_count, slot_count, block_width, _ = near_mats.shape
    skel_rank = interp.shape[2]
    quarters = lax.axis_size("rhs")
    quarter_len = skel_rank * block_count // quarters
    region = lax.axis_index("space")
    onehot = (
        skel_idx[:, :, None] == jnp.arange(block_width, dtype=jnp.int32)[None, None, :]
    ).astype(jnp.float32)
    restrict = onehot + jnp.swapaxes(interp.astype(jnp.float32), 1, 2)
    local_ids = near_ids - (region - 1) * block_count
    live_slots = jnp.arange(slot_count, dtype=jnp.int32)[None, :] < near_count[:, None]
    full_rows = lax.all_gather(coupling, "rhs", axis=1, tiled=True)

    def precond(vector):
        projected = lax.psum(jnp.dot(vector, low_rank, precision=HIGH), "space")
        return diag_prec[None, :] * vector - jnp.dot(projected, low_rank.T, precision=HIGH)

    def operate(field):
        field_low = field.astype(jnp.bfloat16)
        extended = padded(field_low, (("space", 1),), panels)
        blocks = extended.reshape(excitations, 3 * block_count, block_width)
        picked = blocks[:, local_ids] * live_slots[None, :, :, None].astype(jnp.bfloat16)
        near = jnp.einsum("bkij,ebkj->ebi", near_mats, picked, preferred_element_type=jnp.float32)
        own_blocks = field_low.reshape(excitations, block_count, block_width).astype(jnp.float32)
        charges = jnp.einsum("brj,ebj->ebr", restrict, own_blocks, precision=HIGH)
        packed = charges.astype(jnp.bfloat16).reshape(excitations, quarters, quarter_len)
        charges_in = lax.all_gather(packed, "space", axis=2, tiled=True)
        far_field = jnp.einsum(
            "sqc,eqc->es", full_rows, charges_in, preferred_element_type=jnp.float32
        )
        far_pot = jnp.einsum(
            "brj,ebr->ebj",
            restrict,
            far_field.reshape(excitations, block_count, skel_rank),
            precision=HIGH,
        )
        return (
            self_coef[None, :] * field
            + near.reshape(excitations, panels)
            + far_pot.reshape(excitations, panels)
        )

    def orthogonalize(residue, basis_vecs):
        coeffs = lax.psum(
            jnp.stack([column_sum(residue * basis_one) for basis_one in basis_vecs]), "space"
        )
        for index_one in range(len(basis_vecs)):
            residue = residue - coeffs[index_one][:, None] * basis_vecs[index_one]
        length = jnp.sqrt(lax.psum(column_sum(residue * residue), "space") + EPS)
        return (residue, coeffs, length)

    start_len = jnp.sqrt(lax.psum(column_sum(rhs_vec * rhs_vec), "space") + EPS)
    first_dir = rhs_vec / start_len[:, None]
    first_pre = precond(first_dir)
    residue, coeffs_one, below_one = orthogonalize(operate(first_pre), [first_dir])
    second_dir = residue / below_one[:, None]
    second_pre = precond(second_dir)
    residue, coeffs_two, below_two = orthogonalize(operate(second_pre), [first_dir, second_dir])
    step_one, step_two = givens_pair(
        start_len, coeffs_one[0], below_one, coeffs_two[0], coeffs_two[1], below_two
    )
    return step_one[:, None] * first_pre + step_two[:, None] * second_pre


def solution(mesh):
    placed = (
        P("rhs", "space"),
        P("space"),
        P("space", None, None, None),
        P("space", None),
        P("space"),
        P("space", None, None),
        P("space", None),
        P("space", "rhs", None),
        P("space"),
        P("space", None),
    )
    return jax.shard_map(
        on_device, mesh=mesh, in_specs=placed, out_specs=P("rhs", "space"), check_vma=False
    )
```

profile of v0, /device:TPU:1, one launch (start us, length us, event | category | flops | bytes accessed | tf_op | source)
XLA Modules:
  0.0 1282.3 jit_solution(1113078736265904027)
XLA Ops:
  6.5 0.7 all-gather.2.cloned.1.call-update
  7.3 0.3 copy-done.1
  7.5 0.1 multiply_reduce_fusion.5
  7.6 128.3 %psum.49 = f32[16]{0:T(128)S(1)} all-reduce(f32[16]{0:T(128)S(1)} %multiply_reduce_fusion.5), channel_id=1, replica_groups=mesh['space'=64,'rhs'=4] {'space'}, use_global_device_ids=true, to_apply=%region_1.0 | all-reduce | flops 16 | bytes 128 | tf_op jit(solution)/shard_map/psum | solution.py:107
  135.9 0.0 copy-start.4
  135.9 0.0 copy-start.6
  136.0 1.1 fusion.30
  137.1 245.5 %psum.50 = f32[16,512]{1,0:T(8,128)S(1)} all-reduce(f32[16,512]{1,0:T(8,128)S(1)} %fusion.30), channel_id=1, replica_groups=mesh['space'=64,'rhs'=4] {'space'}, use_global_device_ids=true, to_apply=%region_2.0 | all-reduce | flops 8192 | bytes 65536 | tf_op jit(solution)/shard_map/psum | solution.py:70
  382.6 1.8 fusion.31
  384.4 7.6 collective-permute-start.1
  392.0 1.9 collective-permute-start
  393.9 0.3 fusion.4
  394.2 0.1 reshape.72
  394.3 0.1 copy.39
  394.5 0.1 reshape.84
  394.6 54.5 %all_gather.9 = bf16[16,4,4096]{0,1,2:T(4,128)(2,1)} all-gather(bf16[16,4,64]{0,1,2:T(4,128)(2,1)S(1)} %copy.39), channel_id=1, replica_groups=mesh['space'=64,'rhs'=4] {'space'}, dimensions={2}, use_global_device_ids=true | all-gather | bytes 532480 | tf_op jit(solution)/shard_map/all_gather | solution.py:82
  449.0 0.1 fusion.28
  449.1 0.0 collective-permute-done.1
  449.1 0.0 collective-permute-done
  449.1 0.6 gather_fusion
  449.8 2.3 convolution_bitcast_fusion.3
  452.1 6.9 fusion.6
  459.0 0.1 reshape.73
  459.1 0.3 convolution_bitcast_fusion.1
  459.4 0.2 multiply_reduce_fusion.4
  459.6 123.6 %psum.51 = f32[16]{0:T(128)S(1)} all-reduce(f32[16]{0:T(128)S(1)} %get-tuple-element.10), channel_id=1, replica_groups=mesh['space'=64,'rhs'=4] {'space'}, use_global_device_ids=true, to_apply=%region_4.0 | all-reduce | flops 16 | bytes 128 | tf_op jit(solution)/shard_map/psum | solution.py:99
  583.2 0.2 multiply_reduce_fusion.3
  583.4 126.7 %psum.52 = f32[16]{0:T(128)S(1)} all-reduce(f32[16]{0:T(128)S(1)} %multiply_reduce_fusion.3), channel_id=1, replica_groups=mesh['space'=64,'rhs'=4] {'space'}, use_global_device_ids=true, to_apply=%region_6.0 | all-reduce | flops 16 | bytes 128 | tf_op jit(solution)/shard_map/psum | solution.py:104
  710.1 0.1 broadcast_divide_fusion
  710.2 1.1 fusion.33
  711.3 241.3 %psum.53 = f32[16,512]{1,0:T(8,128)S(1)} all-reduce(f32[16,512]{1,0:T(8,128)S(1)} %fusion.33), channel_id=1, replica_groups=mesh['space'=64,'rhs'=4] {'space'}, use_global_device_ids=true, to_apply=%region_7.0 | all-reduce | flops 8192 | bytes 65536 | tf_op jit(solution)/shard_map/psum | solution.py:70
  952.6 1.8 fusion.32
  954.4 0.3 fusion.5
  954.7 7.6 collective-permute-start.3
  962.3 1.9 collective-permute-start.2
  964.2 0.1 reshape.78
  964.3 0.1 copy.47
  964.4 50.4 %all_gather.11 = bf16[16,4,4096]{0,1,2:T(4,128)(2,1)S(1)} all-gather(bf16[16,4,64]{0,1,2:T(4,128)(2,1)S(1)} %copy.47), channel_id=1, replica_groups=mesh['space'=64,'rhs'=4] {'space'}, dimensions={2}, use_global_device_ids=true | all-gather | bytes 532480 | tf_op jit(solution)/shard_map/all_gather | solution.py:82
  1014.9 5.8 fusion.9
  1020.6 0.1 reshape.79
  1020.7 0.3 convolution_bitcast_fusion
  1021.1 0.6 gather_fusion.1
  1021.7 2.3 convolution_bitcast_fusion.2
  1024.0 0.2 multiply_reduce_fusion.2
  1024.2 123.6 %psum.54 = f32[2,16]{1,0:T(2,128)S(1)} all-reduce(f32[2,16]{1,0:T(2,128)S(1)} %pad_maximum_fusion), channel_id=1, replica_groups=mesh['space'=64,'rhs'=4] {'space'}, use_global_device_ids=true, to_apply=%region_10.0 | all-reduce | flops 32 | bytes 256 | tf_op jit(solution)/shard_map/psum | solution.py:99
  1147.8 0.2 multiply_reduce_fusion
  1148.0 126.7 %psum.55 = f32[16]{0:T(128)S(1)} all-reduce(f32[16]{0:T(128)S(1)} %multiply_reduce_fusion), channel_id=1, replica_groups=mesh['space'=64,'rhs'=4] {'space'}, use_global_device_ids=true, to_apply=%region_12.0 | all-reduce | flops 16 | bytes 128 | tf_op jit(solution)/shard_map/psum | solution.py:104
  1274.7 0.7 multiply_add_fusion
  (28 shorter events, 0.2 us)
Async XLA Ops:
  6.5 129.4 %copy-start = (f32[1024,512]{1,0:T(8,128)S(1)}, f32[1024,512]{1,0:T(8,128)}, u32[]{:S(2)}) copy-start(f32[1024,512]{1,0:T(8,128)} %param.19) | copy-start | bytes 6291460
  6.5 1.0 copy-start.1
  6.5 376.0 %copy-start.3 = (f32[1024]{0:T(1024)S(1)}, f32[1024]{0:T(1024)}, u32[]{:S(2)}) copy-start(f32[1024]{0:T(1024)} %param.18) | copy-start | bytes 12292
  6.5 445.5 %all-gather.2.cloned.1.call-start = ((), (), s32[]{:S(2)}) async-start(), calls=%async_computation | async-start | bytes 10485760 | tf_op jit(solution)/shard_map/all_gather | solution.py:67
  135.9 258.0 %copy-start.2 = (bf16[8,128,32]{1,2,0:T(8,128)(2,1)S(1)}, bf16[8,128,32]{1,2,0:T(8,128)(2,1)}, u32[]{:S(2)}) copy-start(bf16[8,128,32]{1,2,0:T(8,128)(2,1)} %param.15) | copy-start | bytes 196612
  135.9 258.0 %copy-start.4 = (s32[8,32]{1,0:T(8,128)S(1)}, s32[8,32]{1,0:T(8,128)}, u32[]{:S(2)}) copy-start(s32[8,32]{1,0:T(8,128)} %param.16) | copy-start | bytes 3076
  135.9 258.5 %copy-start.6 = (s32[8,8]{1,0:T(8,128)S(1)}, s32[8,8]{1,0:T(8,128)}, u32[]{:S(2)}) copy-start(s32[8,8]{1,0:T(8,128)} %param.13) | copy-start | bytes 772
  384.4 64.7 %collective-permute-start.1 = (bf16[16,1024]{1,0:T(8,128)(2,1)S(1)}, bf16[16,1024]{1,0:T(8,128)(2,1)S(1)}, u32[]{:S(2)}, u32[]{:S(2)}) collective-permute-start(bf16[16,1024]{1,0:T(8,128)(2,1)S(1)} %get-tuple-element.14), channel_id=1, source_target_pairs={{4,0},{8,4},{12,8},{16,12},{20,16},{24,20},{28,24},{32,28},{36,32}... | collective-permute-start | bytes 98312 | tf_op jit(solution)/shard_map/ppermute | solution.py:20
  392.0 57.2 %collective-permute-start = (bf16[16,1024]{1,0:T(8,128)(2,1)S(1)}, bf16[16,1024]{1,0:T(8,128)(2,1)S(1)}, u32[]{:S(2)}, u32[]{:S(2)}) collective-permute-start(bf16[16,1024]{1,0:T(8,128)(2,1)S(1)} %get-tuple-element.14), channel_id=1, source_target_pairs={{0,4},{4,8},{8,12},{12,16},{16,20},{20,24},{24,28},{28,32},{32,36}... | collective-permute-start | bytes 98312 | tf_op jit(solution)/shard_map/ppermute | solution.py:18
  394.6 54.5 %copy-start.7 = (s32[8]{0:T(128)S(1)}, s32[8]{0:T(128)}, u32[]{:S(2)}) copy-start(s32[8]{0:T(128)} %param.14) | copy-start | bytes 100
  452.1 7.4 copy-start.5
  954.7 66.3 %collective-permute-start.3 = (bf16[16,1024]{1,0:T(8,128)(2,1)S(1)}, bf16[16,1024]{1,0:T(8,128)(2,1)S(1)}, u32[]{:S(2)}, u32[]{:S(2)}) collective-permute-start(bf16[16,1024]{1,0:T(8,128)(2,1)S(1)} %get-tuple-element.16), channel_id=1, source_target_pairs={{4,0},{8,4},{12,8},{16,12},{20,16},{24,20},{28,24},{32,28},{36,32}... | collective-permute-start | bytes 98312 | tf_op jit(solution)/shard_map/ppermute | solution.py:20
  962.3 58.8 %collective-permute-start.2 = (bf16[16,1024]{1,0:T(8,128)(2,1)S(1)}, bf16[16,1024]{1,0:T(8,128)(2,1)S(1)}, u32[]{:S(2)}, u32[]{:S(2)}) collective-permute-start(bf16[16,1024]{1,0:T(8,128)(2,1)S(1)} %get-tuple-element.16), channel_id=1, source_target_pairs={{0,4},{4,8},{8,12},{12,16},{16,20},{20,24},{24,28},{28,32},{32,36}... | collective-permute-start | bytes 98312 | tf_op jit(solution)/shard_map/ppermute | solution.py:18
Sparse Core Ops, SparseCore 0:
  9.2 89.4 all-gather.1
where the time goes:
time: 1280 us
  blocking collectives  1220 us (95%)
  matrix products  24.4 us (2%)
  starting transfers between devices  19 us (1%)
  between operations  13.6 us (1%)
    psum x2, blocking collectives, precond(): projected = lax.psum(jnp.dot(vector, low_rank, precision=HIGH), 'space')  487 us
    psum x2, blocking collectives, orthogonalize(): length = jnp.sqrt(lax.psum(column_sum(residue * residue), 'space') + EPS)  253 us
    psum x2, blocking collectives, orthogonalize(): lax.psum(jnp.stack([column_sum(residue * basis_one) for basis_one in basi...  247 us
    psum x1, blocking collectives, on_device(): start_len = jnp.sqrt(lax.psum(column_sum(rhs_vec * rhs_vec), 'space') + EPS)  128 us
    all_gather x2, blocking collectives, operate(): charges_in = lax.all_gather(packed, 'space', axis=2, tiled=True)  105 us
  transfers between devices with their start and end apart: 5, of which 0 were waited for; matrix products, arithmetic and copies ran while one was open for 1% of the time, Pallas kernels for 0%

commit v1 on v0

--- a/solution.py
+++ b/solution.py
@@ -79,7 +79,10 @@
         own_blocks = field_low.reshape(excitations, block_count, block_width).astype(jnp.float32)
         charges = jnp.einsum("brj,ebj->ebr", restrict, own_blocks, precision=HIGH)
         packed = charges.astype(jnp.bfloat16).reshape(excitations, quarters, quarter_len)
-        charges_in = lax.all_gather(packed, "space", axis=2, tiled=True)
+        size = lax.axis_size("space")
+        shards = jnp.stack([packed for _ in range(size)])
+        shards = lax.all_to_all(shards, "space", split_axis=0, concat_axis=0)
+        charges_in = jnp.concatenate(shards, axis=2)
         far_field = jnp.einsum(
             "sqc,eqc->es", full_rows, charges_in, preferred_element_type=jnp.float32
         )

time: 1280 us -> 1230 us (0.961)
  blocking collectives: 1220 us -> 1110 us
  waiting for transfers between devices: 0.72 us -> 19 us
  starting transfers between devices: 19 us -> 36.1 us
  local copies, waits for them, and re-layouts: 2.29 us -> 15.3 us
    all_gather x2 -> x0, blocking collectives: 105 us -> none  [operate(): charges_in = lax.all_gather(packed, 'space', axis=2, tiled=True)]
    all_to_all x0 -> x2, starting transfers between devices: none -> 24.8 us  [operate(): shards = lax.all_to_all(shards, 'space', split_axis=0, concat_axis=0)]
    all_to_all x0 -> x2, waiting for transfers between devices: none -> 16.6 us  [operate(): shards = lax.all_to_all(shards, 'space', split_axis=0, concat_axis=0)]
  transfers between devices with their start and end apart: 5 -> 7, of which waited for: 0 -> 5; matrix products, arithmetic and copies ran while one was open for 1% -> 1% of each run, Pallas kernels for 0% -> 0%
where the time goes in v1:
time: 1230 us
  blocking collectives  1110 us (90%)
  starting transfers between devices  36.1 us (3%)
  matrix products  29.8 us (2%)
  waiting for transfers between devices  19 us (2%)
  local copies, waits for them, and re-layouts  15.3 us (1%)
  between operations  13.7 us (1%)
    psum x2, blocking collectives, precond(): projected = lax.psum(jnp.dot(vector, low_rank, precision=HIGH), 'space')  487 us
    psum x2, blocking collectives, orthogonalize(): length = jnp.sqrt(lax.psum(column_sum(residue * residue), 'space') + EPS)  252 us
    psum x2, blocking collectives, orthogonalize(): lax.psum(jnp.stack([column_sum(residue * basis_one) for basis_one in basi...  247 us
    psum x1, blocking collectives, on_device(): start_len = jnp.sqrt(lax.psum(column_sum(rhs_vec * rhs_vec), 'space') + EPS)  128 us
    all_to_all x2, starting transfers between devices, operate(): shards = lax.all_to_all(shards, 'space', split_axis=0, concat_axis=0)  24.8 us
  transfers between devices with their start and end apart: 7, of which 5 were waited for; matrix products, arithmetic and copies ran while one was open for 1% of the time, Pallas kernels for 0%

profile of v1, /device:TPU:1, one launch (start us, length us, event | category | flops | bytes accessed | tf_op | source)
XLA Modules:
  0.0 1229.7 jit_solution(389475474566951855)
XLA Ops:
  6.5 0.7 all-gather.2.cloned.1.call-update
  7.3 0.3 copy-done.1
  7.6 128.3 %psum.49 = f32[16]{0:T(128)S(1)} all-reduce(f32[16]{0:T(128)S(1)} %multiply_reduce_fusion.5), channel_id=1, replica_groups=mesh['space'=64,'rhs'=4] {'space'}, use_global_device_ids=true, to_apply=%region_1.0 | all-reduce | flops 16 | bytes 128 | tf_op jit(solution)/shard_map/psum | solution.py:110
  136.0 1.1 fusion.20
  137.1 245.5 %psum.50 = f32[16,512]{1,0:T(8,128)S(1)} all-reduce(f32[16,512]{1,0:T(8,128)S(1)} %fusion.20), channel_id=1, replica_groups=mesh['space'=64,'rhs'=4] {'space'}, use_global_device_ids=true, to_apply=%region_2.0 | all-reduce | flops 8192 | bytes 65536 | tf_op jit(solution)/shard_map/psum | solution.py:70
  382.6 1.8 fusion.21
  384.4 0.3 fusion
  384.9 0.2 broadcast_bitcast_fusion.1
  385.1 1.6 reshape.118
  386.7 10.5 all-to-all-start
  397.3 2.5 collective-permute-start.1
  399.8 3.2 collective-permute-start
  403.2 0.6 collective-permute-done
  403.9 0.6 gather_fusion
  404.5 2.3 convolution_bitcast_fusion.5
  406.8 8.4 all-to-all-done
  415.1 2.3 reshape.119
  417.6 0.7 copy.50
  418.3 1.7 reshape.111
  420.0 9.1 convolution_bitcast_fusion.1
  429.0 0.3 convolution_bitcast_fusion.3
  429.4 0.2 multiply_reduce_fusion.4
  429.6 123.7 %psum.51 = f32[16]{0:T(128)S(1)} all-reduce(f32[16]{0:T(128)S(1)} %get-tuple-element.10), channel_id=1, replica_groups=mesh['space'=64,'rhs'=4] {'space'}, use_global_device_ids=true, to_apply=%region_4.0 | all-reduce | flops 16 | bytes 128 | tf_op jit(solution)/shard_map/psum | solution.py:102
  553.3 0.2 multiply_reduce_fusion.3
  553.5 125.8 %psum.52 = f32[16]{0:T(128)S(1)} all-reduce(f32[16]{0:T(128)S(1)} %multiply_reduce_fusion.3), channel_id=1, replica_groups=mesh['space'=64,'rhs'=4] {'space'}, use_global_device_ids=true, to_apply=%region_6.0 | all-reduce | flops 16 | bytes 128 | tf_op jit(solution)/shard_map/psum | solution.py:107
  679.4 1.1 fusion.23
  680.5 241.1 %psum.53 = f32[16,512]{1,0:T(8,128)S(1)} all-reduce(f32[16,512]{1,0:T(8,128)S(1)} %fusion.23), channel_id=1, replica_groups=mesh['space'=64,'rhs'=4] {'space'}, use_global_device_ids=true, to_apply=%region_7.0 | all-reduce | flops 8192 | bytes 65536 | tf_op jit(solution)/shard_map/psum | solution.py:70
  921.6 1.8 fusion.22
  923.5 0.3 fusion.1
  923.9 0.2 broadcast_bitcast_fusion
  924.1 1.6 reshape.120
  925.8 14.3 %all-to-all-start.1 = ((bf16[64,2,2048]{2,1,0:T(2,128)(2,1)}), bf16[64,2,2048]{2,1,0:T(2,128)(2,1)}, u32[]{:S(2)}, u32[]{:S(2)}) async-start(bf16[64,2,2048]{2,1,0:T(2,128)(2,1)} %reshape.120), calls=%async_computation.1 | async-start | bytes 1048576 | tf_op jit(solution)/shard_map/all_to_all | solution.py:84
  940.1 2.4 collective-permute-start.3
  942.5 3.1 collective-permute-start.2
  945.7 0.4 collective-permute-done.3
  946.1 0.6 collective-permute-done.2
  946.7 0.6 gather_fusion.1
  947.3 2.3 convolution_bitcast_fusion.4
  949.6 8.3 all-to-all-done.1
  957.8 2.3 reshape.121
  960.3 0.7 copy.58
  961.0 1.7 reshape.114
  962.7 9.1 convolution_bitcast_fusion
  971.8 0.3 convolution_bitcast_fusion.2
  972.3 123.7 %psum.54 = f32[2,16]{1,0:T(2,128)S(1)} all-reduce(f32[2,16]{1,0:T(2,128)S(1)} %pad_maximum_fusion), channel_id=1, replica_groups=mesh['space'=64,'rhs'=4] {'space'}, use_global_device_ids=true, to_apply=%region_10.0 | all-reduce | flops 32 | bytes 256 | tf_op jit(solution)/shard_map/psum | solution.py:102
  1096.0 0.2 multiply_reduce_fusion
  1096.2 125.8 %psum.55 = f32[16]{0:T(128)S(1)} all-reduce(f32[16]{0:T(128)S(1)} %multiply_reduce_fusion), channel_id=1, replica_groups=mesh['space'=64,'rhs'=4] {'space'}, use_global_device_ids=true, to_apply=%region_12.0 | all-reduce | flops 16 | bytes 128 | tf_op jit(solution)/shard_map/psum | solution.py:107
  1222.1 0.7 multiply_add_fusion
  (52 shorter events, 1.3 us)
Async XLA Ops:
  6.5 129.4 %copy-start = (f32[1024,512]{1,0:T(8,128)S(1)}, f32[1024,512]{1,0:T(8,128)}, u32[]{:S(2)}) copy-start(f32[1024,512]{1,0:T(8,128)} %param.19) | copy-start | bytes 6291460
  6.5 1.0 copy-start.1
  6.5 376.0 %copy-start.3 = (f32[1024]{0:T(1024)S(1)}, f32[1024]{0:T(1024)}, u32[]{:S(2)}) copy-start(f32[1024]{0:T(1024)} %param.18) | copy-start | bytes 12292
  6.5 413.4 %all-gather.2.cloned.1.call-start = ((), (), s32[]{:S(2)}) async-start(), calls=%async_computation.2 | async-start | bytes 10485760 | tf_op jit(solution)/shard_map/all_gather | solution.py:67
  135.9 248.5 %copy-start.10 = (f32[16]{0:T(128)}, f32[16]{0:T(128)S(1)}, u32[]{:S(2)}) copy-start(f32[16]{0:T(128)S(1)} %psum.49) | copy-start | bytes 196
  135.9 248.5 %copy-start.2 = (bf16[8,128,32]{1,2,0:T(8,128)(2,1)S(1)}, bf16[8,128,32]{1,2,0:T(8,128)(2,1)}, u32[]{:S(2)}) copy-start(bf16[8,128,32]{1,2,0:T(8,128)(2,1)} %param.15) | copy-start | bytes 196612
  135.9 248.5 %copy-start.4 = (s32[8,32]{1,0:T(8,128)S(1)}, s32[8,32]{1,0:T(8,128)}, u32[]{:S(2)}) copy-start(s32[8,32]{1,0:T(8,128)} %param.16) | copy-start | bytes 3076
  384.4 18.6 %copy-start.8 = (s32[8,8]{1,0:T(8,128)S(1)}, s32[8,8]{1,0:T(8,128)}, u32[]{:S(2)}) copy-start(s32[8,8]{1,0:T(8,128)} %param.13) | copy-start | bytes 772
  384.4 18.7 %copy-start.9 = (s32[8]{0:T(128)S(1)}, s32[8]{0:T(128)}, u32[]{:S(2)}) copy-start(s32[8]{0:T(128)} %param.14) | copy-start | bytes 100
  386.7 28.4 %all-to-all-start = ((bf16[64,2,2048]{2,1,0:T(2,128)(2,1)}), bf16[64,2,2048]{2,1,0:T(2,128)(2,1)}, u32[]{:S(2)}, u32[]{:S(2)}) async-start(bf16[64,2,2048]{2,1,0:T(2,128)(2,1)} %reshape.118), calls=%async_computation | async-start | bytes 1048576 | tf_op jit(solution)/shard_map/all_to_all | solution.py:84
  397.3 5.9 collective-permute-start.1
  399.8 4.0 collective-permute-start
  420.0 9.4 copy-start.5
  553.3 370.2 %copy-start.6 = (f32[16]{0:T(128)}, f32[16]{0:T(128)S(1)}, u32[]{:S(2)}) copy-start(f32[16]{0:T(128)S(1)} %psum.51) | copy-start | bytes 196
  679.3 244.2 %copy-start.12 = (f32[16]{0:T(128)}, f32[16]{0:T(128)S(1)}, u32[]{:S(2)}) copy-start(f32[16]{0:T(128)S(1)} %psum.52) | copy-start | bytes 196
  925.8 32.1 %all-to-all-start.1 = ((bf16[64,2,2048]{2,1,0:T(2,128)(2,1)}), bf16[64,2,2048]{2,1,0:T(2,128)(2,1)}, u32[]{:S(2)}, u32[]{:S(2)}) async-start(bf16[64,2,2048]{2,1,0:T(2,128)(2,1)} %reshape.120), calls=%async_computation.1 | async-start | bytes 1048576 | tf_op jit(solution)/shard_map/all_to_all | solution.py:84
  940.1 6.0 collective-permute-start.3
  942.5 4.1 collective-permute-start.2
  962.7 259.4 %copy-start.7 = (f32[16]{0:T(128)S(1)}, f32[16]{0:T(128)}, u32[]{:S(2)}) copy-start(f32[16]{0:T(128)} %copy-done.6) | copy-start | bytes 196
  962.7 259.4 %copy-start.11 = (f32[16]{0:T(128)S(1)}, f32[16]{0:T(128)}, u32[]{:S(2)}) copy-start(f32[16]{0:T(128)} %copy-done.10) | copy-start | bytes 196
  962.7 259.4 %copy-start.13 = (f32[16]{0:T(128)S(1)}, f32[16]{0:T(128)}, u32[]{:S(2)}) copy-start(f32[16]{0:T(128)} %copy-done.12) | copy-start | bytes 196
Sparse Core Ops, SparseCore 0:
  9.2 89.4 all-gather.1
